TPU v7x, 32 devices: a whole 2x2x4 slice. The times are simulated.
32 devices in a mesh: lat: 16 (over z, x, core), chan: 2 (over y).
Axes of the slice: x: 2, y: 2, z: 4, core: 2. Of those that a mesh axis runs over, the one named last changes fastest.
Arguments:
- ocean_state: bfloat16 [384, 256, 1440], P('lat', 'chan'), may hold values from -6 to 6
- land_mask: int32 [384, 1440], P('lat', 'chan'), may hold values 0 or 1
- order_table: int32 [384], replicated, may hold values from 0 to 383, each once
- spectral_weight: bfloat16 [384, 2, 256, 256], P('lat', None, 'chan'), may hold values from -0.25 to 0.25
- inner_weight: bfloat16 [256, 512], P(None, 'chan'), may hold values from -0.375 to 0.375
- outer_weight: bfloat16 [512, 256], P('chan'), may hold values from -0.25 to 0.25
Outputs:
- layer_output: bfloat16 [384, 1440, 256], P('lat', 'chan')
Inputs may be any that keep to these rules, and one draw needn't show every extreme that they name: `order_table`: a permutation: every order from 0 to 383 stands in exactly one slot.
All inputs are finite; a program needn't handle non-finite values. Where the computation divides by a largest or mean magnitude, that divisor is 1e-20 or more. No bound on the sum of `land_mask` on one device may be relied on, other than what follows from the above.
Results may differ from a plain program's by a relative error of at most 0.0095.
Values may be sent and summed in bfloat16 or wider, within the bound.
No kernel may reach another device: no remote copies, remote signals or barrier semaphores. Data moves between devices by JAX's collectives and lax.ppermute only.
A program may use at most 128 MiB of HBM per device.

v0:
```python
import math
import jax
import jax.numpy as jnp
from jax import lax
from jax.sharding import PartitionSpec as P

NLAT = 384
NLON = 1440
MODES = 384


def fejer_weights():
    colatitude = (jnp.arange(NLAT, dtype=jnp.float32) + 0.5) * (math.pi / NLAT)
    harmonic = jnp.arange(1, NLAT // 2 + 1).astype(jnp.float32)
    series = (
        jnp.cos(2.0 * colatitude[:, None] * harmonic[None, :])
        / (4.0 * harmonic * harmonic - 1.0)[None, :]
    )
    return 2.0 / NLAT * (1.0 - 2.0 * jnp.sum(series, axis=1))


def compose(earlier, latter):
    first_mat, first_log = earlier
    second_mat, second_log = latter
    product = jnp.stack(
        [
            second_mat[0] * first_mat[0] + second_mat[1] * first_mat[2],
            second_mat[0] * first_mat[1] + second_mat[1] * first_mat[3],
            second_mat[2] * first_mat[0] + second_mat[3] * first_mat[2],
            second_mat[2] * first_mat[1] + second_mat[3] * first_mat[3],
        ]
    )
    largest = jnp.max(jnp.abs(product), axis=0, keepdims=True)
    return (product / largest, first_log + second_log + jnp.log(largest))


def legendre_rows(order_value):
    half_rows = NLAT // 2
    colatitude = (jnp.arange(half_rows, dtype=jnp.float32) + 0.5) * (math.pi / NLAT)
    cosine = jnp.cos(colatitude)
    sine_part = jnp.sin(colatitude)
    offsets = jnp.arange(MODES).astype(jnp.float32)
    order_float = order_value.astype(jnp.float32)
    degree = order_float + offsets
    beyond_start = offsets >= 1.0
    denominator = jnp.where(beyond_start, degree * degree - order_float * order_float, 1.0)
    upper_coef = jnp.sqrt((4.0 * degree * degree - 1.0) / denominator)
    previous = degree - 1.0
    lower_coef = jnp.sqrt(
        jnp.maximum(previous * previous - order_float * order_float, 0.0)
        / jnp.maximum(4.0 * previous * previous - 1.0, 1.0)
    )
    filled = jnp.ones((MODES, half_rows), jnp.float32)
    beyond_column = beyond_start[:, None]
    matrix = jnp.stack(
        [
            jnp.where(beyond_column, upper_coef[:, None] * cosine[None, :], filled),
            jnp.where(beyond_column, -(upper_coef * lower_coef)[:, None] * filled, 0.0 * filled),
            jnp.where(beyond_column, filled, 0.0 * filled),
            jnp.where(beyond_column, 0.0 * filled, filled),
        ]
    )
    log_scale = jnp.zeros((1, MODES, half_rows), jnp.float32)
    matrix, log_scale = lax.associative_scan(compose, (matrix, log_scale), axis=1)
    steps_log = 0.5 * jnp.log((2.0 * offsets + 3.0) / (2.0 * offsets + 2.0))
    cumulative = jnp.cumsum(steps_log) - steps_log
    picked = jnp.sum(jnp.where(jnp.arange(MODES) == order_value, cumulative, 0.0 * cumulative))
    start_log = 0.5 * math.log(0.5) + picked + order_float * jnp.log(sine_part)
    northern = jnp.exp(start_log[None, :] + log_scale[0]) * matrix[0]
    northern = jnp.where((offsets < MODES - order_float)[:, None], northern, 0.0 * filled)
    parity = jnp.where(jnp.arange(MODES) % 2 == 0, 1.0, -1.0).astype(jnp.float32)
    return jnp.concatenate([northern, northern[:, ::-1] * parity[:, None]], axis=1)


def fourier_tables(orders):
    longitude = jnp.arange(NLON)
    phase_index = orders[:, None] * longitude[None, :] % NLON
    angles = phase_index.astype(jnp.float32) * (2.0 * math.pi / NLON)
    cosine = jnp.cos(angles)
    sine_part = jnp.sin(angles)
    forward = (
        jnp.concatenate([cosine, -sine_part], axis=0) * (math.sqrt(2.0 * math.pi) / NLON)
    ).astype(jnp.bfloat16)
    factor = jnp.where(orders == 0, 1.0, 2.0).astype(jnp.float32) / math.sqrt(2.0 * math.pi)
    inverse = jnp.concatenate(
        [cosine * factor[:, None], -sine_part * factor[:, None]], axis=0
    ).astype(jnp.bfloat16)
    return (forward, inverse)


def mixing_blocks(weights):
    real_part = weights[:, 0]
    imag_part = weights[:, 1]
    return jnp.stack(
        [jnp.stack([real_part, imag_part], axis=1), jnp.stack([-imag_part, real_part], axis=1)],
        axis=1,
    )


def local(ocean_state, land_mask, order_table, spectral_weight, inner_weight, outer_weight):
    local_rows = ocean_state.shape[0]
    local_channels = ocean_state.shape[1]
    slots_here = spectral_weight.shape[0]
    forward, inverse = fourier_tables(order_table)
    flat_state = ocean_state.reshape(local_rows * local_channels, NLON)
    coeffs = lax.dot_general(
        flat_state, forward, (((1,), (1,)), ((), ())), preferred_element_type=jnp.float32
    )
    coeffs = coeffs.astype(jnp.bfloat16).reshape(local_rows, local_channels, 2, MODES)
    owned_coeffs = lax.all_to_all(coeffs, "lat", split_axis=3, concat_axis=0, tiled=True)
    first_slot = lax.axis_index("lat") * slots_here
    my_orders = lax.dynamic_slice_in_dim(order_table, first_slot, slots_here)
    tables = lax.map(legendre_rows, my_orders)
    weighted = (tables * fejer_weights()[None, None, :]).astype(jnp.bfloat16)
    plain_table = tables.astype(jnp.bfloat16)
    spectra = jnp.einsum(
        "rcpm,mkr->mpck", owned_coeffs, weighted, preferred_element_type=jnp.float32
    ).astype(jnp.bfloat16)
    gathered = lax.all_gather(spectra, "chan", axis=2, tiled=True)
    blocks = mixing_blocks(spectral_weight)
    mixed_spec = jnp.einsum(
        "mpck,mpqdc->mqdk", gathered, blocks, preferred_element_type=jnp.float32
    ).astype(jnp.bfloat16)
    synthesis = jnp.einsum(
        "mqdk,mkr->rdqm", mixed_spec, plain_table, preferred_element_type=jnp.float32
    ).astype(jnp.bfloat16)
    rows_back = lax.all_to_all(synthesis, "lat", split_axis=0, concat_axis=3, tiled=True)
    spatial = jnp.dot(
        rows_back.reshape(local_rows * local_channels, 2 * MODES),
        inverse,
        preferred_element_type=jnp.float32,
    )
    spatial = spatial.reshape(local_rows, local_channels, NLON)
    hidden = (ocean_state.astype(jnp.float32) + spatial).astype(jnp.bfloat16)
    points = lax.all_to_all(hidden, "chan", split_axis=2, concat_axis=1, tiled=True)
    inner_full, outer_full = (
        lax.all_gather(inner_weight, "chan", axis=1, tiled=True),
        lax.all_gather(outer_weight, "chan", axis=0, tiled=True),
    )
    pre_act = jnp.einsum("rcp,ch->rph", points, inner_full, preferred_element_type=jnp.float32)
    activated = jax.nn.gelu(pre_act).astype(jnp.bfloat16)
    update = jnp.einsum("rph,hc->rpc", activated, outer_full, preferred_element_type=jnp.float32)
    ocean_mask = land_mask.astype(jnp.float32)
    residual_part = jnp.transpose(points, (0, 2, 1)).astype(jnp.float32)
    return (ocean_mask[:, :, None] * (residual_part + update)).astype(jnp.bfloat16)


def solution(mesh):
    placed = (
        P("lat", "chan", None),
        P("lat", "chan"),
        P(),
        P("lat", None, "chan", None),
        P(None, "chan"),
        P("chan", None),
    )
    return jax.shard_map(
        local, mesh=mesh, in_specs=placed, out_specs=P("lat", "chan", None), check_vma=False
    )
```

profile of v0, /device:TPU:0, one launch (start us, length us, event | category | flops | bytes accessed | tf_op | source)
XLA Modules:
  0.0 1467.7 jit_solution(10121995507402593260)
XLA Ops:
  7.2 11.2 multiply_convert_fusion.2
  18.4 10.6 fusion.83
  29.0 3.6 copy.80
  32.6 11.8 copy.57
  44.3 7.4 all-to-all-start
  53.2 932.7 %while.13 = (s32[]{:T(128)}, f32[24,384,384]{2,1,0:T(8,128)}, s32[24]{0:T(128)}, s32[]{:T(128)}, f32[]{:T(128)}, /*index=5*/f32[]{:T(128)}, f32[]{:T(128)}) while((s32[]{:T(128)}, f32[24,384,384]{2,1,0:T(8,128)}, s32[24]{0:T(128)}, s32[]{:T(128)}, f32[]{:T(128)}, /*index=5*/f32[]{:T(128)}, f32[]{:T(128)}) %tuple.122), condition=%wide.region_20.21_spmd, body=%wide.region_0.20_spmd.sunk | while | flops 9975949 | bytes 54367292 | solution.py:113
  73.2 2.9 pad.1097
  112.0 2.9 pad.1097
  150.9 2.9 pad.1097
  267.4 2.9 pad.1097
  306.3 2.9 pad.1097
  383.9 2.9 pad.1097
  422.8 2.9 pad.1097
  772.5 2.9 pad.1097
  850.1 2.9 pad.1097
  889.0 2.9 pad.1097
  987.1 3.6 copy.58
  990.6 3.4 copy.59
  994.0 11.3 convert_bitcast_fusion.1
  1009.5 115.3 %all-gather.2.cloned.1.call-done = bf16[24,2,256,384]{2,3,1,0:T(8,128)(2,1)} async-done(((bf16[24,2,128,384]{2,3,1,0:T(8,128)(2,1)}), bf16[24,2,256,384]{2,3,1,0:T(8,128)(2,1)}) %all-gather.2.cloned.1.call-update) | async-done | bytes 9437200 | tf_op jit(solution)/shard_map/all_gather | solution.py:119
  1124.8 10.3 fusion.55
  1135.0 11.7 convert_bitcast_fusion
  1146.7 9.4 copy.63
  1156.1 108.9 %all_to_all.51 = bf16[384,128,2,24]{1,2,3,0:T(2,128)(2,1)S(1)} all-to-all(bf16[384,128,2,24]{1,2,3,0:T(2,128)(2,1)} %copy.63), channel_id=1, replica_groups=mesh['lat'=16,'chan'=2] {'lat'}, dimensions={0} | all-to-all | bytes 9437184 | tf_op jit(solution)/shard_map/all_to_all | solution.py:127
  1267.2 9.6 add_convert_fusion
  1276.9 16.9 %copy.67 = bf16[24,128,1440]{1,0,2:T(8,128)(2,1)} copy(bf16[24,128,1440]{1,2,0:T(8,128)(2,1)S(1)} %add_convert_fusion) | data formatting | bytes 17694720 | tf_op jit(solution)/shard_map/convert_element_type | solution.py:134
  1293.7 7.2 all-to-all-start.2
  1301.0 101.3 %all_gather.10 = bf16[256,512]{1,0:T(8,128)(2,1)S(1)} all-gather(bf16[256,256]{1,0:T(8,128)(2,1)S(1)} %copy-done.19), channel_id=1, replica_groups=mesh['lat'=16,'chan'=2] {'chan'}, dimensions={1}, use_global_device_ids=true | all-gather | bytes 393216 | tf_op jit(solution)/shard_map/all_gather | solution.py:137
  1402.3 6.2 all_gather.11
  1408.5 14.2 copy.102
  1422.7 20.0 %all_to_all.47 = bf16[24,256,720]{1,2,0:T(8,128)(2,1)} reshape(bf16[24,2,128,720]{2,1,3,0:T(2,128)(2,1)} %bitcast.169) | data formatting | bytes 17694720 | tf_op jit(solution)/shard_map/all_to_all | solution.py:135
  1442.7 18.0 %fusion.52 = bf16[24,720,256]{2,1,0:T(8,128)(2,1)} fusion(bf16[24,256,720]{1,2,0:T(8,128)(2,1)} %all_to_all.47, f32[24,720]{1,0:T(8,128)S(1)} %convert_element_type.124, bf16[512,256]{1,0:T(8,128)(2,1)S(1)} %all_gather.11, bf16[256,512]{1,0:T(8,128)(2,1)S(1)} %all_gather.10), kind=kOutput, calls=%fused_computation.239 | convolution fusion | flops 9157017600 | bytes 18288128 | tf_op jit(solution)/shard_map/rph,hc->rpc/dot_general | solution.py:142
  (5779 shorter events, 854.6 us)
Async XLA Ops:
  44.3 942.7 %all-to-all-start = ((bf16[24,128,2,384]{1,2,0,3:T(2,128)(2,1)}), bf16[24,128,2,384]{1,2,0,3:T(2,128)(2,1)}, u32[]{:S(2)}, u32[]{:S(2)}) async-start(bf16[24,128,2,384]{1,2,0,3:T(2,128)(2,1)} %copy.57), calls=%async_computation | async-start | bytes 9437184 | tf_op jit(solution)/shard_map/all_to_all | solution.py:110
  51.8 1073.0 %all-gather.2.cloned.1.call-start = ((), (), s32[]{:S(2)}) async-start(), calls=%async_computation.3 | async-start | bytes 14155776 | tf_op jit(solution)/shard_map/all_gather | solution.py:119
  73.1 3.4 copy-start.1
  76.2 10.2 copy-start.4
  115.0 10.2 copy-start.4
  150.7 3.4 copy-start.1
  153.8 10.2 copy-start.4
  192.7 10.2 copy-start.4
  231.5 10.2 copy-start.4
  270.4 10.2 copy-start.4
  309.2 10.2 copy-start.4
  348.1 10.2 copy-start.4
  386.9 10.2 copy-start.4
  425.7 10.2 copy-start.4
  464.6 10.2 copy-start.4
  503.4 10.2 copy-start.4
  542.3 10.2 copy-start.4
  581.1 10.2 copy-start.4
  620.0 10.2 copy-start.4
  658.9 10.2 copy-start.4
  697.8 10.2 copy-start.4
  736.6 10.2 copy-start.4
  775.4 10.2 copy-start.4
  814.3 10.2 copy-start.4
  853.1 10.2 copy-start.4
  891.9 10.2 copy-start.4
  930.8 10.2 copy-start.4
  969.7 10.2 copy-start.4
  1293.7 7.2 copy-start.21
  1293.7 7.3 copy-start.19
  1293.7 108.6 %copy-start.20 = (bf16[256,256]{1,0:T(8,128)(2,1)S(1)}, bf16[256,256]{1,0:T(8,128)(2,1)}, u32[]{:S(2)}) copy-start(bf16[256,256]{1,0:T(8,128)(2,1)} %param.13) | copy-start | bytes 393220
  1293.7 114.8 %all-to-all-start.2 = ((bf16[24,128,1440]{1,0,2:T(8,128)(2,1)}), bf16[24,128,1440]{1,0,2:T(8,128)(2,1)}, u32[]{:S(2)}, u32[]{:S(2)}) async-start(bf16[24,128,1440]{1,0,2:T(8,128)(2,1)} %copy.67), calls=%async_computation.2 | async-start | bytes 17694720 | tf_op jit(solution)/shard_map/all_to_all | solution.py:135
  (361 other events, 284.4 us)
Sparse Core Ops, SparseCore 0:
  1005.5 119.2 all-gather.1
where the time goes:
time: 1490 us; the launch traced here: 1470 us
  local copies, waits for them, and re-layouts  563 us (38%)
  other arithmetic  414 us (28%)
  blocking collectives  216 us (14%)
  waiting for transfers between devices  115 us (8%)
  matrix products  71.4 us (5%)
  loops' own time  59 us (4%)
    while x840, local copies, waits for them, and re-layouts  257 us
    add x336, other arithmetic, compose(): return (product / largest, first_log + second_log + jnp.log(largest))  183 us
    all_gather x1, waiting for transfers between devices, local(): gathered = lax.all_gather(spectra, 'chan', axis=2, tiled=True)  115 us
    slice x1272, local copies, waits for them, and re-layouts, legendre_rows(): lax.associative_scan(compose, (matrix, log_scale), axis=1)  115 us
    all_to_all x1, blocking collectives, local(): lax.all_to_all(synthesis, 'lat', split_axis=0, concat_axis=3, tiled=True)  109 us
    all_gather x1, blocking collectives, local(): lax.all_gather(inner_weight, 'chan', axis=1, tiled=True)  101 us
    another operation x1, loops' own time, local(): tables = lax.map(legendre_rows, my_orders)  59 us
    add x384, other arithmetic, compose(): second_mat[0] * first_mat[0] + second_mat[1] * first_mat[2]  44.1 us

commit v1 on v0

--- a/solution.py
+++ b/solution.py
@@ -7,6 +7,21 @@
 NLAT = 384
 NLON = 1440
 MODES = 384
+
+
+def _settle_copies(frame_in, row_axis, mat):
+    k_now = lax.axis_size(row_axis)
+    everything = lax.axis_index(row_axis)
+    finding, tile_out = (k_now, everything)
+    samples = [(b, (b - 1) % finding) for b in range(finding)]
+    x_new = frame_in.shape[2]
+    b_now = frame_in
+    last = mat(b_now, tile_out * x_new)
+    for k0 in tuple(range(1, finding)):
+        b_now = lax.ppermute(b_now, perm=samples, axis_name=row_axis)
+        all_values = mat(b_now, (tile_out + k0) % finding * x_new)
+        last = last + all_values
+    return last
 
 
 def fejer_weights():
@@ -116,10 +131,16 @@
     spectra = jnp.einsum(
         "rcpm,mkr->mpck", owned_coeffs, weighted, preferred_element_type=jnp.float32
     ).astype(jnp.bfloat16)
-    gathered = lax.all_gather(spectra, "chan", axis=2, tiled=True)
     blocks = mixing_blocks(spectral_weight)
-    mixed_spec = jnp.einsum(
-        "mpck,mpqdc->mqdk", gathered, blocks, preferred_element_type=jnp.float32
+    mixed_spec = _settle_copies(
+        spectra,
+        "chan",
+        lambda part, at: jnp.einsum(
+            "mpck,mpqdc->mqdk",
+            part,
+            lax.dynamic_slice_in_dim(blocks, at, part.shape[2], axis=4),
+            preferred_element_type=jnp.float32,
+        ),
     ).astype(jnp.bfloat16)
     synthesis = jnp.einsum(
         "mqdk,mkr->rdqm", mixed_spec, plain_table, preferred_element_type=jnp.float32

time: 1490 us -> 1460 us (0.980)
  waiting for transfers between devices: 115 us -> 92.7 us
    all_gather x1 -> x0, waiting for transfers between devices: 115 us -> none  [local(): gathered = lax.all_gather(spectra, 'chan', axis=2, tiled=True)]
    ppermute x0 -> x1, waiting for transfers between devices: none -> 92.7 us  [_settle_copies(): b_now = lax.ppermute(b_now, perm=samples, axis_name=row_axis)]
where the time goes in v1:
time: 1460 us; the launch traced here: 1440 us
  local copies, waits for them, and re-layouts  555 us (38%)
  other arithmetic  417 us (29%)
  blocking collectives  217 us (15%)
  waiting for transfers between devices  92.7 us (6%)
  matrix products  76.6 us (5%)
  loops' own time  62.9 us (4%)
  starting transfers between devices  16.7 us (1%)
    while x840, local copies, waits for them, and re-layouts  260 us
    add x336, other arithmetic, compose(): return (product / largest, first_log + second_log + jnp.log(largest))  184 us
    slice x1272, local copies, waits for them, and re-layouts, legendre_rows(): lax.associative_scan(compose, (matrix, log_scale), axis=1)  115 us
    all_to_all x1, blocking collectives, local(): lax.all_to_all(synthesis, 'lat', split_axis=0, concat_axis=3, tiled=True)  109 us
    all_gather x1, blocking collectives, local(): lax.all_gather(inner_weight, 'chan', axis=1, tiled=True)  101 us
    ppermute x1, waiting for transfers between devices, _settle_copies(): b_now = lax.ppermute(b_now, perm=samples, axis_name=row_axis)  92.7 us
    another operation x1, loops' own time, local(): tables = lax.map(legendre_rows, my_orders)  62.9 us
    add x384, other arithmetic, compose(): second_mat[0] * first_mat[0] + second_mat[1] * first_mat[2]  44.1 us

profile of v1, /device:TPU:0, one launch (start us, length us, event | category | flops | bytes accessed | tf_op | source)
XLA Modules:
  0.0 1438.4 jit_solution(4020693393407691791)
XLA Ops:
  0.7 11.2 multiply_convert_fusion.2
  11.8 10.2 fusion.90
  23.4 3.0 copy.47
  26.4 8.0 all-to-all-start
  35.8 943.1 %while.13 = (s32[]{:T(128)}, f32[24,384,384]{2,1,0:T(8,128)}, s32[24]{0:T(128)}, s32[]{:T(128)}, f32[]{:T(128)}, /*index=5*/f32[]{:T(128)}, f32[]{:T(128)}) while((s32[]{:T(128)}, f32[24,384,384]{2,1,0:T(8,128)}, s32[24]{0:T(128)}, s32[]{:T(128)}, f32[]{:T(128)}, /*index=5*/f32[]{:T(128)}, f32[]{:T(128)}) %tuple.125), condition=%wide.region_20.21_spmd, body=%wide.region_0.20_spmd.sunk | while | flops 9975949 | bytes 54367292 | solution.py:128
  55.7 2.9 pad.1103
  95.0 2.9 pad.1103
  134.3 2.9 pad.1103
  173.6 2.9 pad.1103
  252.2 2.9 pad.1103
  291.4 2.9 pad.1103
  370.0 2.9 pad.1103
  409.3 2.9 pad.1103
  762.9 2.9 pad.1103
  841.5 2.9 pad.1103
  880.8 2.9 pad.1103
  980.0 5.9 copy.48
  985.8 11.2 fusion.87
  1003.5 5.4 fusion.75
  1008.9 92.7 %collective-permute-done = bf16[24,2,128,384]{2,3,1,0:T(8,128)(2,1)} collective-permute-done((bf16[24,2,128,384]{2,3,1,0:T(8,128)(2,1)}, bf16[24,2,128,384]{2,3,1,0:T(8,128)(2,1)}, u32[]{:S(2)}, u32[]{:S(2)}) %collective-permute-start) | collective-permute-done | bytes 4718624 | tf_op jit(solution)/shard_map/ppermute | solution.py:21
  1101.6 7.8 fusion.73
  1109.4 14.4 %convert_bitcast_fusion = bf16[384,128,2,24]{1,0,2,3:T(8,128)(2,1)} fusion(f32[24,384,384]{2,1,0:T(8,128)} %get-tuple-element.65, f32[24,2,128,384,1]{3,2,1,0,4:T(8,128)} %fusion.73, f32[24,2,128,384,1]{3,2,1,0,4:T(8,128)} %fusion.75), kind=kOutput, calls=%fused_computation.266 | convolution fusion | flops 1822556160 | bytes 37748736 | tf_op jit(solution)/shard_map/mqdk,mkr->rdqm/dot_general | solution.py:145
  1123.8 9.3 copy.53
  1133.1 109.0 %all_to_all.51 = bf16[384,128,2,24]{1,2,3,0:T(2,128)(2,1)S(1)} all-to-all(bf16[384,128,2,24]{1,2,3,0:T(2,128)(2,1)} %copy.53), channel_id=1, replica_groups=mesh['lat'=16,'chan'=2] {'lat'}, dimensions={0} | all-to-all | bytes 9437184 | tf_op jit(solution)/shard_map/all_to_all | solution.py:148
  1244.4 9.6 add_convert_fusion
  1254.0 16.9 %copy.57 = bf16[24,128,1440]{1,0,2:T(8,128)(2,1)} copy(bf16[24,128,1440]{1,2,0:T(8,128)(2,1)S(1)} %add_convert_fusion) | data formatting | bytes 17694720 | tf_op jit(solution)/shard_map/convert_element_type | solution.py:155
  1270.9 7.2 all-to-all-start.2
  1278.2 101.3 %all_gather.6 = bf16[256,512]{1,0:T(8,128)(2,1)S(1)} all-gather(bf16[256,256]{1,0:T(8,128)(2,1)S(1)} %copy-done.18), channel_id=1, replica_groups=mesh['lat'=16,'chan'=2] {'chan'}, dimensions={1}, use_global_device_ids=true | all-gather | bytes 393216 | tf_op jit(solution)/shard_map/all_gather | solution.py:158
  1379.5 6.2 all_gather.7
  1385.6 14.3 copy.105
  1400.0 20.0 %all_to_all.47 = bf16[24,256,720]{1,2,0:T(8,128)(2,1)} reshape(bf16[24,2,128,720]{2,1,3,0:T(2,128)(2,1)} %bitcast.183) | data formatting | bytes 17694720 | tf_op jit(solution)/shard_map/all_to_all | solution.py:156
  1419.9 18.0 %fusion.52 = bf16[24,720,256]{2,1,0:T(8,128)(2,1)} fusion(bf16[24,256,720]{1,2,0:T(8,128)(2,1)} %all_to_all.47, f32[24,720]{1,0:T(8,128)S(1)} %convert_element_type.124, bf16[512,256]{1,0:T(8,128)(2,1)S(1)} %all_gather.7, bf16[256,512]{1,0:T(8,128)(2,1)S(1)} %all_gather.6), kind=kOutput, calls=%fused_computation.239 | convolution fusion | flops 9157017600 | bytes 18288128 | tf_op jit(solution)/shard_map/rph,hc->rpc/dot_general | solution.py:163
  (5783 shorter events, 861.0 us)
Async XLA Ops:
  26.4 953.5 %all-to-all-start = ((bf16[24,128,2,384]{1,0,2,3:T(8,128)(2,1)}), bf16[24,128,2,384]{1,0,2,3:T(8,128)(2,1)}, u32[]{:S(2)}, u32[]{:S(2)}) async-start(bf16[24,128,2,384]{1,0,2,3:T(8,128)(2,1)} %copy.47), calls=%async_computation | async-start | bytes 9437184 | tf_op jit(solution)/shard_map/all_to_all | solution.py:125
  55.6 3.5 copy-start.1
  58.8 10.2 copy-start.4
  98.0 10.2 copy-start.4
  134.2 3.5 copy-start.1
  137.3 10.2 copy-start.4
  176.6 10.2 copy-start.4
  215.9 10.2 copy-start.4
  255.2 10.2 copy-start.4
  294.5 10.2 copy-start.4
  333.7 10.2 copy-start.4
  373.0 10.2 copy-start.4
  412.3 10.2 copy-start.4
  451.6 10.2 copy-start.4
  490.9 10.2 copy-start.4
  530.2 10.2 copy-start.4
  569.4 10.2 copy-start.4
  608.7 10.2 copy-start.4
  648.1 10.2 copy-start.4
  687.4 10.2 copy-start.4
  726.7 10.2 copy-start.4
  766.0 10.2 copy-start.4
  805.2 10.2 copy-start.4
  844.5 10.2 copy-start.4
  883.8 10.2 copy-start.4
  923.1 10.2 copy-start.4
  962.4 10.2 copy-start.4
  997.1 104.5 %collective-permute-start = (bf16[24,2,128,384]{2,3,1,0:T(8,128)(2,1)}, bf16[24,2,128,384]{2,3,1,0:T(8,128)(2,1)}, u32[]{:S(2)}, u32[]{:S(2)}) collective-permute-start(bf16[24,2,128,384]{2,3,1,0:T(8,128)(2,1)} %bitcast.180), channel_id=1, source_target_pairs={{0,1},{1,0},{2,3},{3,2},{4,5},{5,4},{6,7},{7,6},{8,9},{9,8},{10,11... | collective-permute-start | bytes 14155784 | tf_op jit(solution)/shard_map/ppermute | solution.py:21
  1270.9 7.2 copy-start.20
  1270.9 7.3 copy-start.18
  1270.9 108.6 %copy-start.19 = (bf16[256,256]{1,0:T(8,128)(2,1)S(1)}, bf16[256,256]{1,0:T(8,128)(2,1)}, u32[]{:S(2)}) copy-start(bf16[256,256]{1,0:T(8,128)(2,1)} %param.13) | copy-start | bytes 393220
  1270.9 114.8 %all-to-all-start.2 = ((bf16[24,128,1440]{1,0,2:T(8,128)(2,1)}), bf16[24,128,1440]{1,0,2:T(8,128)(2,1)}, u32[]{:S(2)}, u32[]{:S(2)}) async-start(bf16[24,128,1440]{1,0,2:T(8,128)(2,1)} %copy.57), calls=%async_computation.2 | async-start | bytes 17694720 | tf_op jit(solution)/shard_map/all_to_all | solution.py:156
  (362 other events, 288.8 us)
